TPU v7x, 32 devices: a whole 2x2x4 slice. The times are simulated.
32 devices in a mesh: pipe: 8 (over z, y), head: 4 (over x, core).
Axes of the slice: x: 2, y: 2, z: 4, core: 2. Of those that a mesh axis runs over, the one named last changes fastest.
Arguments:
- queries: bfloat16 [2, 2048, 8192], P(None, 'pipe', 'head'), may hold values from -150 to 150
- keys: bfloat16 [2048, 1024], P(('pipe', 'head')), may hold values from -7 to 7
- values: bfloat16 [2048, 1024], P(('pipe', 'head')), may hold values from -6 to 6
- slice_index: int32 [2, 8], replicated, may hold values from 0 to 7, each once within a row
Outputs:
- attended: bfloat16 [2, 2048, 8192], P(None, 'pipe', 'head')
Inputs may be any that keep to these rules, and one draw needn't show every extreme that they name: Each row of slice_index is a permutation of 0 to 7.
All inputs are finite; a program needn't handle non-finite values.
Results may differ from a plain program's by a relative error of at most 0.0041.
Values may be sent and summed in bfloat16 or wider, within the bound.
A program may use at most 128 MiB of HBM per device.

v0:
```python
import math

import jax
import jax.numpy as jnp
from jax import lax
from jax.experimental import pallas as pl
from jax.experimental.pallas import tpu as pltpu
from jax.sharding import PartitionSpec as P

HEAD_SIZE = 128
NEG = -1e30
TO_EXP2 = HEAD_SIZE ** (-0.5) * math.log2(math.e)
PAIRS = 2
UNROLL = 8


def scores_of(query, key_block):
    return lax.dot_general(query, key_block, (((1,), (1,)), ((), ())), preferred_element_type=jnp.float32)


def weigh(scores, peak, value_block):
    weights = jnp.exp2((scores - peak) * TO_EXP2).astype(jnp.bfloat16)
    ones = jnp.ones(value_block.shape, jnp.bfloat16)
    return jnp.dot(weights, jnp.concatenate([value_block, ones], axis=1), preferred_element_type=jnp.float32)


MESH = pl.DeviceIdType.MESH


def fused_kernel(n_pipe, n_head, index_ref, q_ref, k_ref, v_ref, o_ref, kbuf, vbuf, qbuf, obuf, best_ref, accum_ref, local_sem, head_send, head_recv, left_send, right_send, side_send, chunk_recv, q_sem, out_sem):
    me = lax.axis_index("pipe")
    head = lax.axis_index("head")
    side = me + 1 - 2 * lax.rem(me, 2)
    row = lax.div(me, 2)
    line = n_pipe // 2
    has_left, has_right = row > 0, row < line - 1
    piece = k_ref.shape[0]
    rows = piece * n_head
    width = kbuf.shape[1]
    ins, bufs = (k_ref, v_ref), (kbuf, vbuf)

    barrier = pltpu.get_barrier_semaphore()
    for other in range(1, n_head):
        pl.semaphore_signal(barrier, inc=1, device_id=(me, lax.rem(head + other, n_head)), device_id_type=MESH)
    pl.semaphore_signal(barrier, inc=1, device_id=(side, head), device_id_type=MESH)

    @pl.when(has_left)
    def _():
        pl.semaphore_signal(barrier, inc=1, device_id=(me - 2, head), device_id_type=MESH)

    @pl.when(has_right)
    def _():
        pl.semaphore_signal(barrier, inc=1, device_id=(me + 2, head), device_id_type=MESH)

    pl.semaphore_wait(barrier, n_head + jnp.where(has_left, 1, 0) + jnp.where(has_right, 1, 0))

    def chunk(kind, owner):
        return bufs[kind].at[pl.ds(pl.multiple_of(owner * rows, rows), rows), :]

    def spot(kind, source):
        return bufs[kind].at[pl.ds(pl.multiple_of(me * rows + source * piece, piece), piece), :]

    def columns(kind, target):
        return ins[kind].at[:, pl.ds(pl.multiple_of(target * width, width), width)]

    def exchange(kind, other):
        return pltpu.make_async_remote_copy(
            columns(kind, lax.rem(head + other, n_head)), spot(kind, head),
            head_send.at[kind, other], head_recv.at[kind, other],
            device_id=(me, lax.rem(head + other, n_head)), device_id_type=MESH)

    def arrival(kind, other):
        source = lax.rem(head + n_head - other, n_head)
        return pltpu.make_async_remote_copy(
            columns(kind, head), spot(kind, source),
            head_send.at[kind, other], head_recv.at[kind, other],
            device_id=(me, source), device_id_type=MESH)

    def pass_on(kind, owner, target, sems):
        return pltpu.make_async_remote_copy(
            chunk(kind, owner), chunk(kind, owner), sems.at[kind, owner], chunk_recv.at[kind, owner],
            device_id=(target, head), device_id_type=MESH)

    def to_left(kind, owner):
        return pass_on(kind, owner, me - 2, left_send)

    def to_right(kind, owner):
        return pass_on(kind, owner, me + 2, right_send)

    def to_side(kind, owner):
        return pass_on(kind, owner, side, side_send)

    for kind in range(2):
        for other in range(1, n_head):
            exchange(kind, other).start()
        pltpu.make_async_copy(columns(kind, head), spot(kind, head), local_sem.at[kind]).start()
    pltpu.make_async_copy(q_ref, qbuf, q_sem).start()
    for kind in range(2):
        pltpu.make_async_copy(columns(kind, head), spot(kind, head), local_sem.at[kind]).wait()
        for other in range(1, n_head):
            arrival(kind, other).wait_recv()
        to_side(kind, me).start()

        @pl.when(has_left)
        def _():
            to_left(kind, me).start()

        @pl.when(has_right)
        def _():
            to_right(kind, me).start()

    def handle(step):
        for kind in range(2):

            @pl.when(row >= step)
            def _():
                owner = me - 2 * step
                to_right(kind, owner).wait_recv()
                to_side(kind, owner).start()

                @pl.when(has_right)
                def _():
                    to_right(kind, owner).start()

            @pl.when(row + step < line)
            def _():
                owner = me + 2 * step
                to_left(kind, owner).wait_recv()
                to_side(kind, owner).start()

                @pl.when(has_left)
                def _():
                    to_left(kind, owner).start()

    ticks, _, q_width = qbuf.shape
    heads = width // HEAD_SIZE
    group = q_width // width
    batches = group // UNROLL
    strip = UNROLL * HEAD_SIZE
    bodies = ticks * heads * batches
    pair_rows = 2 * rows
    steps = line // PAIRS
    diff = lax.broadcasted_iota(jnp.int32, (rows, pair_rows), 1) - lax.broadcasted_iota(jnp.int32, (rows, pair_rows), 0)
    reach = jnp.minimum(row, line - 1 - row)

    def nearest(place):
        offset = lax.div(place + 1, 2)
        near = jnp.where(lax.rem(place, 2) == 1, row - offset, row + offset)
        far = jnp.where(row < line - 1 - row, place, line - 1 - place)
        return jnp.where(place <= 2 * reach, near, far)

    def strip_out(item):
        tick = lax.div(item, heads * batches)
        at = pl.ds(pl.multiple_of(lax.rem(item, heads * batches) * strip, strip), strip)
        return pltpu.make_async_copy(obuf.at[tick, :, at], o_ref.at[tick, :, at], out_sem.at[item])

    def wide(array, count):
        return jnp.concatenate([array] * count, axis=1)

    def compute(step, first, last):
        pairs = [nearest(step * PAIRS + at) for at in range(PAIRS)]
        for pair in pairs:
            for kind in range(2):
                to_side(kind, 2 * pair + lax.rem(side, 2)).wait_recv()
        spans = [pl.ds(pl.multiple_of(pair * pair_rows, pair_rows), pair_rows) for pair in pairs]

        @pl.loop(0, bodies)
        def _(item):
            if not last:
                for at in range(PAIRS):
                    later = (step + 1) * PAIRS + at

                    @pl.when(item == (1 + 3 * at) * bodies // 8)
                    def _():
                        handle(later)

            tick = lax.div(item, heads * batches)
            strip_at = lax.rem(item, heads * batches)
            kv = pl.ds(pl.multiple_of(lax.div(strip_at, batches) * HEAD_SIZE, HEAD_SIZE), HEAD_SIZE)
            start = index_ref[tick, me] * rows
            for u in range(UNROLL):
                at = pl.ds(pl.multiple_of(strip_at * strip + u * HEAD_SIZE, HEAD_SIZE), HEAD_SIZE)
                slot = item * UNROLL + u
                query = qbuf[tick, :, at]
                scores = jnp.concatenate([
                    jnp.where(diff <= start - pair * pair_rows, scores_of(query, kbuf[span, kv]), NEG)
                    for pair, span in zip(pairs, spans)
                ], axis=1)
                top = jnp.broadcast_to(jnp.max(scores, axis=-1, keepdims=True), (rows, HEAD_SIZE))
                if first:
                    peak = top
                else:
                    before = best_ref[slot]
                    peak = jnp.maximum(before, top)
                block = jnp.concatenate([vbuf[span, kv] for span in spans], axis=0)
                result = weigh(scores, wide(peak, PAIRS * pair_rows // HEAD_SIZE), block)
                if not first:
                    result = result + accum_ref[slot] * wide(jnp.exp2((before - peak) * TO_EXP2), 2)
                if last:
                    obuf[tick, :, at] = (result[:, :HEAD_SIZE] / result[:, HEAD_SIZE:]).astype(obuf.dtype)
                else:
                    best_ref[slot] = peak
                    accum_ref[slot] = result
            if last:
                strip_out(item).start()

    handle(1)
    pltpu.make_async_copy(q_ref, qbuf, q_sem).wait()
    compute(0, True, steps == 1)
    if steps > 2:

        @pl.loop(1, steps - 1)
        def _(step):
            compute(step, False, False)

    if steps > 1:
        compute(steps - 1, False, True)

    for kind in range(2):
        for other in range(1, n_head):
            exchange(kind, other).wait_send()

    @pl.loop(0, line)
    def _(index):
        for kind in range(2):
            owner = 2 * index + lax.rem(me, 2)
            to_side(kind, owner).wait_send()

            @pl.when(jnp.logical_and(has_right, index <= row))
            def _():
                to_right(kind, owner).wait_send()

            @pl.when(jnp.logical_and(has_left, index >= row))
            def _():
                to_left(kind, owner).wait_send()

    @pl.loop(0, bodies)
    def _(item):
        strip_out(item).wait()


def on_device(sizes, queries, keys, values, slice_index):
    n_pipe, n_head = sizes
    ticks, rows, columns = queries.shape
    shape = (rows * n_pipe, keys.shape[1] // n_head)
    slots = ticks * columns // HEAD_SIZE
    whole = pl.BlockSpec(memory_space=pltpu.VMEM)
    anywhere = pl.BlockSpec(memory_space=pl.ANY)
    dma = pltpu.SemaphoreType.DMA
    return pl.pallas_call(
        lambda *refs: fused_kernel(n_pipe, n_head, *refs),
        out_shape=jax.ShapeDtypeStruct(queries.shape, queries.dtype),
        in_specs=[pl.BlockSpec(memory_space=pltpu.SMEM), anywhere, whole, whole],
        out_specs=anywhere,
        scratch_shapes=[
            pltpu.VMEM(shape, keys.dtype),
            pltpu.VMEM(shape, keys.dtype),
            pltpu.VMEM(queries.shape, queries.dtype),
            pltpu.VMEM(queries.shape, queries.dtype),
            pltpu.VMEM((slots, rows, HEAD_SIZE), jnp.float32),
            pltpu.VMEM((slots, rows, 2 * HEAD_SIZE), jnp.float32),
            dma((2,)),
            dma((2, n_head)),
            dma((2, n_head)),
            dma((2, n_pipe)),
            dma((2, n_pipe)),
            dma((2, n_pipe)),
            dma((2, n_pipe)),
            dma,
            dma((slots // UNROLL,)),
        ],
        compiler_params=pltpu.CompilerParams(collective_id=0, has_side_effects=True, vmem_limit_bytes=60 * 2 ** 20),
        name="fused",
    )(slice_index, queries, keys, values)


def solution(mesh):
    sizes = (mesh.shape["pipe"], mesh.shape["head"])
    return jax.shard_map(
        lambda *arrays: on_device(sizes, *arrays),
        mesh=mesh,
        in_specs=(
            P(None, "pipe", "head"),
            P(("pipe", "head"), None),
            P(("pipe", "head"), None),
            P(),
        ),
        out_specs=P(None, "pipe", "head"),
        check_vma=False,
    )
```

profile of v0, /device:TPU:0, one launch (start us, length us, event | category | flops | bytes accessed | tf_op | source)
XLA Modules:
  0.0 56.4 jit_solution(2124371044938052432)
XLA Ops:
  0.0 53.2 %fused.1 = bf16[2,256,2048]{2,1,0:T(8,128)(2,1)} custom-call(s32[2,8]{1,0:T(2,128)} %refs_0_.1, bf16[2,256,2048]{2,1,0:T(8,128)(2,1)} %refs_1_.1, bf16[64,1024]{1,0:T(8,128)(2,1)} %refs_2_.1, bf16[64,1024]{1,0:T(8,128)(2,1)} %refs_3_.1), custom_call_target="tpu_custom_call" | custom-call | tf_op jit(solution)/shard_map/fused/pallas_call | solution.py:250
  53.2 3.2 %copy.6 = bf16[2,256,2048]{2,1,0:T(8,128)(2,1)} copy(bf16[2,256,2048]{2,1,0:T(8,128)(2,1)} %fused.1) | data formatting | bytes 4194304
where the time goes:
time: 56.5 us; the launch traced here: 56.4 us
  Pallas kernels  53.2 us (94%)
  local copies, waits for them, and re-layouts  3.16 us (6%)
    pallas_call x1, Pallas kernels, on_device(): pl.pallas_call(lambda *refs: fused_kernel(n_pipe, n_head, *refs), out_sha...  53.2 us
    unnamed x1, local copies, waits for them, and re-layouts  3.16 us

commit v1 on v0

v1 whole, which is shorter than its diff:
```python
import math

import jax
import jax.numpy as jnp
from jax import lax
from jax.experimental import pallas as pl
from jax.experimental.pallas import tpu as pltpu
from jax.sharding import PartitionSpec as P

HEAD_SIZE = 128
NEG = -1e30
TO_EXP2 = HEAD_SIZE ** (-0.5) * math.log2(math.e)
MESH = pl.DeviceIdType.MESH
STRIP = 4


def scores_of(query, key_block):
    return lax.dot_general(query, key_block, (((1,), (1,)), ((), ())), preferred_element_type=jnp.float32)


def weigh(scores, peak, value_block):
    weights = jnp.exp2((scores - peak) * TO_EXP2).astype(jnp.bfloat16)
    ones = jnp.ones(value_block.shape, jnp.bfloat16)
    return jnp.dot(weights, jnp.concatenate([value_block, ones], axis=1), preferred_element_type=jnp.float32)


def wide(array, count):
    return jnp.concatenate([array] * count, axis=1)


def fused_kernel(n_pipe, n_head, index_ref, q_ref, k_ref, v_ref, o_ref, kbuf, vbuf, qbuf, obuf, best_ref, accum_ref,
                 local_sem, head_send, head_recv, left_send, right_send, side_send, chunk_recv, q_sem, out_sem):
    me = lax.axis_index("pipe")
    head = lax.axis_index("head")
    side = me + 1 - 2 * lax.rem(me, 2)
    row = lax.div(me, 2)
    line = n_pipe // 2
    has_left, has_right = row > 0, row < line - 1
    piece = k_ref.shape[0]
    rows = piece * n_head
    near_heads = n_head // 2
    half_rows = rows // 2
    mine = lax.div(head, near_heads)
    width = kbuf.shape[1]
    ins, bufs = (k_ref, v_ref), (kbuf, vbuf)

    barrier = pltpu.get_barrier_semaphore()
    for other in range(1, n_head):
        pl.semaphore_signal(barrier, inc=1, device_id=(me, lax.rem(head + other, n_head)), device_id_type=MESH)
    pl.semaphore_signal(barrier, inc=1, device_id=(side, head), device_id_type=MESH)

    @pl.when(has_left)
    def _():
        pl.semaphore_signal(barrier, inc=1, device_id=(me - 2, head), device_id_type=MESH)

    @pl.when(has_right)
    def _():
        pl.semaphore_signal(barrier, inc=1, device_id=(me + 2, head), device_id_type=MESH)

    def spot(kind, source):
        return bufs[kind].at[pl.ds(pl.multiple_of(me * rows + source * piece, piece), piece), :]

    def columns(kind, target):
        return ins[kind].at[:, pl.ds(pl.multiple_of(target * width, width), width)]

    def keep(kind):
        return pltpu.make_async_copy(columns(kind, head), spot(kind, head), local_sem.at[kind])

    for kind in range(2):
        keep(kind).start()
    pltpu.make_async_copy(q_ref, qbuf, q_sem).start()
    pl.semaphore_wait(barrier, n_head + jnp.where(has_left, 1, 0) + jnp.where(has_right, 1, 0))

    def chunk(kind, owner, half):
        return bufs[kind].at[pl.ds(pl.multiple_of(owner * rows + half * half_rows, half_rows), half_rows), :]

    def partner(far, shift):
        group = lax.rem(mine + far, 2)
        return group * near_heads + lax.rem(lax.rem(head, near_heads) + shift, near_heads)

    def exchange(kind, far, shift):
        target = partner(far, shift)
        return pltpu.make_async_remote_copy(
            columns(kind, target), spot(kind, head),
            head_send.at[kind, far, shift], head_recv.at[kind, far, shift],
            device_id=(me, target), device_id_type=MESH)

    def arrival(kind, far, shift):
        source = partner(far, near_heads - shift)
        return pltpu.make_async_remote_copy(
            columns(kind, head), spot(kind, source),
            head_send.at[kind, far, shift], head_recv.at[kind, far, shift],
            device_id=(me, source), device_id_type=MESH)

    def pass_on(kind, owner, half, target, sems):
        return pltpu.make_async_remote_copy(
            chunk(kind, owner, half), chunk(kind, owner, half), sems.at[kind, owner, half], chunk_recv.at[kind, owner, half],
            device_id=(target, head), device_id_type=MESH)

    def to_left(kind, owner, half):
        return pass_on(kind, owner, half, me - 2, left_send)

    def to_right(kind, owner, half):
        return pass_on(kind, owner, half, me + 2, right_send)

    def to_side(kind, owner, half):
        return pass_on(kind, owner, half, side, side_send)

    for kind in range(2):
        for shift in range(1, near_heads):
            exchange(kind, 0, shift).start()
    for kind in range(2):
        for shift in range(near_heads):
            exchange(kind, 1, shift).start()

    def spread(kind, half):
        to_side(kind, me, half).start()

        @pl.when(has_left)
        def _():
            to_left(kind, me, half).start()

        @pl.when(has_right)
        def _():
            to_right(kind, me, half).start()

    for kind in range(2):
        keep(kind).wait()
        for shift in range(1, near_heads):
            arrival(kind, 0, shift).wait_recv()
        spread(kind, mine)
    for kind in range(2):
        for shift in range(near_heads):
            arrival(kind, 1, shift).wait_recv()
        spread(kind, 1 - mine)

    def halves(order):
        return mine if order == 0 else 1 - mine

    def relay(distance, order):
        half = halves(order)
        has_before, has_after = row >= distance, row + distance < line
        before, after = me - 2 * distance, me + 2 * distance

        @pl.when(has_before)
        def _():
            for kind in range(2):
                to_right(kind, before, half).wait_recv()

                @pl.when(has_right)
                def _():
                    to_right(kind, before, half).start()

                to_side(kind, before, half).start()

        @pl.when(has_after)
        def _():
            for kind in range(2):
                to_left(kind, after, half).wait_recv()

                @pl.when(has_left)
                def _():
                    to_left(kind, after, half).start()

        if order == 0:

            @pl.when(jnp.logical_and(has_after, jnp.logical_not(has_before)))
            def _():
                for kind in range(2):
                    to_side(kind, after, half).start()
        else:

            @pl.when(has_after)
            def _():
                @pl.when(has_before)
                def _():
                    for kind in range(2):
                        to_side(kind, after, mine).start()

                for kind in range(2):
                    to_side(kind, after, half).start()

    ticks, _, q_width = qbuf.shape
    heads = q_width // HEAD_SIZE
    kv_heads = width // HEAD_SIZE
    group = heads // kv_heads
    diff = lax.broadcasted_iota(jnp.int32, (rows, rows), 1) - lax.broadcasted_iota(jnp.int32, (rows, rows), 0)
    reach = jnp.minimum(row, line - 1 - row)

    def nearest(place):
        offset = lax.div(place + 1, 2)
        near = jnp.where(lax.rem(place, 2) == 1, row - offset, row + offset)
        far = jnp.where(row < line - 1 - row, place, line - 1 - place)
        return jnp.where(place <= 2 * reach, near, far)

    strips = heads // STRIP

    def strip_out(tick, strip):
        at = pl.ds(strip * STRIP * HEAD_SIZE, STRIP * HEAD_SIZE)
        return pltpu.make_async_copy(obuf.at[tick, :, at], o_ref.at[tick, :, at], out_sem.at[tick, strip])

    def compute(chunks, first, last, before_tick):
        spans = [pl.ds(pl.multiple_of(owner * rows, rows), rows) for owner in chunks]

        @pl.loop(0, ticks)
        def _(tick):
            before_tick(tick)
            start = index_ref[tick, me] * rows
            for h in range(heads):
                at = pl.ds(h * HEAD_SIZE, HEAD_SIZE)
                kv = pl.ds(h // group * HEAD_SIZE, HEAD_SIZE)
                slot = tick * heads + h
                query = qbuf[tick, :, at]
                scores = wide_join([
                    jnp.where(diff <= start - owner * rows, scores_of(query, kbuf[span, kv]), NEG)
                    for owner, span in zip(chunks, spans)
                ], 1)
                top = jnp.broadcast_to(jnp.max(scores, axis=-1, keepdims=True), (rows, HEAD_SIZE))
                if first:
                    peak = top
                else:
                    before = best_ref[slot]
                    peak = jnp.maximum(before, top)
                block = wide_join([vbuf[span, kv] for span in spans], 0)
                result = weigh(scores, wide(peak, len(chunks) * rows // HEAD_SIZE), block)
                if not first:
                    result = result + accum_ref[slot] * wide(jnp.exp2((before - peak) * TO_EXP2), 2)
                if last:
                    obuf[tick, :, at] = (result[:, :HEAD_SIZE] / result[:, HEAD_SIZE:]).astype(obuf.dtype)
                    if h % STRIP == STRIP - 1:
                        strip_out(tick, h // STRIP).start()
                else:
                    best_ref[slot] = peak
                    accum_ref[slot] = result

    def side_owner(place):
        return 2 * nearest(place) + lax.rem(side, 2)

    def own_owner(place):
        return 2 * nearest(place) + lax.rem(me, 2)

    def side_wait(owner):
        for half in range(2):
            for kind in range(2):
                to_side(kind, owner, half).wait_recv()

    def first_events(tick):
        @pl.when(tick == 0)
        def _():
            relay(1, 0)

    relay_at = first_events
    pltpu.make_async_copy(q_ref, qbuf, q_sem).wait()
    compute([me], True, False, relay_at)

    @pl.loop(1, line)
    def _(step):
        def events(tick):
            @pl.when(tick == 0)
            def _():
                relay(step, 1)
                side_wait(side_owner(step - 1))

            @pl.when(tick == 1)
            def _():
                relay(step + 1, 0)

        compute([own_owner(step), side_owner(step - 1)], False, False, events)

    def last_events(tick):
        @pl.when(tick == 0)
        def _():
            side_wait(side_owner(line - 1))

    compute([side_owner(line - 1)], False, True, last_events)

    for kind in range(2):
        for shift in range(1, near_heads):
            exchange(kind, 0, shift).wait_send()
        for shift in range(near_heads):
            exchange(kind, 1, shift).wait_send()

    @pl.loop(0, line)
    def _(index):
        owner = 2 * index + lax.rem(me, 2)
        for half in range(2):
            for kind in range(2):
                to_side(kind, owner, half).wait_send()

                @pl.when(jnp.logical_and(has_right, index <= row))
                def _():
                    to_right(kind, owner, half).wait_send()

                @pl.when(jnp.logical_and(has_left, index >= row))
                def _():
                    to_left(kind, owner, half).wait_send()

    for tick in range(ticks):
        for strip in range(strips):
            strip_out(tick, strip).wait()


def wide_join(parts, axis):
    return parts[0] if len(parts) == 1 else jnp.concatenate(parts, axis=axis)


def on_device(sizes, queries, keys, values, slice_index):
    n_pipe, n_head = sizes
    ticks, rows, columns = queries.shape
    shape = (rows * n_pipe, keys.shape[1] // n_head)
    slots = ticks * columns // HEAD_SIZE
    anywhere = pl.BlockSpec(memory_space=pl.ANY)
    dma = pltpu.SemaphoreType.DMA
    return pl.pallas_call(
        lambda *refs: fused_kernel(n_pipe, n_head, *refs),
        out_shape=jax.ShapeDtypeStruct(queries.shape, queries.dtype),
        in_specs=[pl.BlockSpec(memory_space=pltpu.SMEM), anywhere, anywhere, anywhere],
        out_specs=anywhere,
        scratch_shapes=[
            pltpu.VMEM(shape, keys.dtype),
            pltpu.VMEM(shape, keys.dtype),
            pltpu.VMEM(queries.shape, queries.dtype),
            pltpu.VMEM(queries.shape, queries.dtype),
            pltpu.VMEM((slots, rows, HEAD_SIZE), jnp.float32),
            pltpu.VMEM((slots, rows, 2 * HEAD_SIZE), jnp.float32),
            dma((2,)),
            dma((2, 2, n_head // 2)),
            dma((2, 2, n_head // 2)),
            dma((2, n_pipe, 2)),
            dma((2, n_pipe, 2)),
            dma((2, n_pipe, 2)),
            dma((2, n_pipe, 2)),
            dma,
            dma((ticks, columns // HEAD_SIZE // STRIP)),
        ],
        compiler_params=pltpu.CompilerParams(collective_id=0, has_side_effects=True, vmem_limit_bytes=60 * 2 ** 20),
        name="fused",
    )(slice_index, queries, keys, values)


def solution(mesh):
    sizes = (mesh.shape["pipe"], mesh.shape["head"])
    return jax.shard_map(
        lambda *arrays: on_device(sizes, *arrays),
        mesh=mesh,
        in_specs=(
            P(None, "pipe", "head"),
            P(("pipe", "head"), None),
            P(("pipe", "head"), None),
            P(),
        ),
        out_specs=P(None, "pipe", "head"),
        check_vma=False,
    )
```

time: 56.5 us -> 42.5 us (0.75)
  Pallas kernels: 53.2 us -> 39.2 us
    pallas_call x1, Pallas kernels: 53.2 us -> 39.2 us  [on_device(): pl.pallas_call(lambda *refs: fused_kernel(n_pipe, n_head, *refs), out_sha...]
where the time goes in v1:
time: 42.5 us; the launch traced here: 42.4 us
  Pallas kernels  39.2 us (92%)
  local copies, waits for them, and re-layouts  3.16 us (7%)
    pallas_call x1, Pallas kernels, on_device(): pl.pallas_call(lambda *refs: fused_kernel(n_pipe, n_head, *refs), out_sha...  39.2 us
    unnamed x1, local copies, waits for them, and re-layouts  3.16 us

profile of v1, /device:TPU:0, one launch (start us, length us, event | category | flops | bytes accessed | tf_op | source)
XLA Modules:
  0.0 42.4 jit_solution(18227104316752604742)
XLA Ops:
  0.0 39.2 %fused.1 = bf16[2,256,2048]{2,1,0:T(8,128)(2,1)} custom-call(s32[2,8]{1,0:T(2,128)} %refs_0_.1, bf16[2,256,2048]{2,1,0:T(8,128)(2,1)} %refs_1_.1, bf16[64,1024]{1,0:T(8,128)(2,1)} %refs_2_.1, bf16[64,1024]{1,0:T(8,128)(2,1)} %refs_3_.1), custom_call_target="tpu_custom_call" | custom-call | tf_op jit(solution)/shard_map/fused/pallas_call | solution.py:314
  39.2 3.2 %copy.6 = bf16[2,256,2048]{2,1,0:T(8,128)(2,1)} copy(bf16[2,256,2048]{2,1,0:T(8,128)(2,1)} %fused.1) | data formatting | bytes 4194304

commit v2 on v1

--- a/solution.py
+++ b/solution.py
@@ -28,8 +28,8 @@
     return jnp.concatenate([array] * count, axis=1)
 
 
-def fused_kernel(n_pipe, n_head, index_ref, q_ref, k_ref, v_ref, o_ref, kbuf, vbuf, qbuf, obuf, best_ref, accum_ref,
-                 local_sem, head_send, head_recv, left_send, right_send, side_send, chunk_recv, q_sem, out_sem):
+def fused_kernel(n_pipe, n_head, slice_ref, q_ref, k_ref, v_ref, o_ref, kbuf, vbuf, qbuf, obuf, best_ref, accum_ref,
+                 index_ref, index_sem, local_sem, head_send, head_recv, left_send, right_send, side_send, chunk_recv, q_sem, out_sem):
     me = lax.axis_index("pipe")
     head = lax.axis_index("head")
     side = me + 1 - 2 * lax.rem(me, 2)
@@ -68,6 +68,7 @@
 
     for kind in range(2):
         keep(kind).start()
+    pltpu.make_async_copy(slice_ref, index_ref, index_sem).start()
     pltpu.make_async_copy(q_ref, qbuf, q_sem).start()
     pl.semaphore_wait(barrier, n_head + jnp.where(has_left, 1, 0) + jnp.where(has_right, 1, 0))
 
@@ -137,6 +138,12 @@
     def halves(order):
         return mine if order == 0 else 1 - mine
 
+    def is_end(at):
+        return jnp.logical_or(at == 0, at == line - 1)
+
+    def crosses(at, order):
+        return True if order == 0 else jnp.logical_or(jnp.logical_not(is_end(at)), at == row)
+
     def relay(distance, order):
         half = halves(order)
         has_before, has_after = row >= distance, row + distance < line
@@ -151,7 +158,9 @@
                 def _():
                     to_right(kind, before, half).start()
 
-                to_side(kind, before, half).start()
+                @pl.when(crosses(row - distance, order))
+                def _():
+                    to_side(kind, before, half).start()
 
         @pl.when(has_after)
         def _():
@@ -170,15 +179,47 @@
                     to_side(kind, after, half).start()
         else:
 
-            @pl.when(has_after)
-            def _():
-                @pl.when(has_before)
-                def _():
-                    for kind in range(2):
-                        to_side(kind, after, mine).start()
-
+            @pl.when(jnp.logical_and(has_after, has_before))
+            def _():
+                for kind in range(2):
+                    to_side(kind, after, mine).start()
+
+            @pl.when(jnp.logical_and(has_after, crosses(row + distance, order)))
+            def _():
                 for kind in range(2):
                     to_side(kind, after, half).start()
+
+    first_side, last_side = lax.rem(side, 2), 2 * (line - 1) + lax.rem(side, 2)
+
+    def guests_start():
+        for kind in range(2):
+
+            @pl.when(row == 0)
+            def _():
+                to_right(kind, first_side, 1 - mine).start()
+
+            @pl.when(row == line - 1)
+            def _():
+                to_left(kind, last_side, 1 - mine).start()
+
+    def guests_pass(distance):
+        for kind in range(2):
+
+            @pl.when(row == distance)
+            def _():
+                to_right(kind, first_side, 1 - mine).wait_recv()
+
+                @pl.when(has_right)
+                def _():
+                    to_right(kind, first_side, 1 - mine).start()
+
+            @pl.when(row == line - 1 - distance)
+            def _():
+                to_left(kind, last_side, 1 - mine).wait_recv()
+
+                @pl.when(has_left)
+                def _():
+                    to_left(kind, last_side, 1 - mine).start()
 
     ticks, _, q_width = qbuf.shape
     heads = q_width // HEAD_SIZE
@@ -240,9 +281,12 @@
         return 2 * nearest(place) + lax.rem(me, 2)
 
     def side_wait(owner):
-        for half in range(2):
-            for kind in range(2):
-                to_side(kind, owner, half).wait_recv()
+        for order in range(2):
+
+            @pl.when(crosses(lax.div(owner, 2), order))
+            def _():
+                for kind in range(2):
+                    to_side(kind, owner, halves(order)).wait_recv()
 
     def first_events(tick):
         @pl.when(tick == 0)
@@ -250,6 +294,7 @@
             relay(1, 0)
 
     relay_at = first_events
+    pltpu.make_async_copy(slice_ref, index_ref, index_sem).wait()
     pltpu.make_async_copy(q_ref, qbuf, q_sem).wait()
     compute([me], True, False, relay_at)
 
@@ -261,6 +306,14 @@
                 relay(step, 1)
                 side_wait(side_owner(step - 1))
 
+                @pl.when(step == 1)
+                def _():
+                    guests_start()
+
+                @pl.when(step > 1)
+                def _():
+                    guests_pass(step - 1)
+
             @pl.when(tick == 1)
             def _():
                 relay(step + 1, 0)
@@ -271,6 +324,7 @@
         @pl.when(tick == 0)
         def _():
             side_wait(side_owner(line - 1))
+            guests_pass(line - 1)
 
     compute([side_owner(line - 1)], False, True, last_events)
 
@@ -283,9 +337,13 @@
     @pl.loop(0, line)
     def _(index):
         owner = 2 * index + lax.rem(me, 2)
-        for half in range(2):
+        for order in range(2):
+            half = halves(order)
             for kind in range(2):
-                to_side(kind, owner, half).wait_send()
+
+                @pl.when(crosses(index, order))
+                def _():
+                    to_side(kind, owner, half).wait_send()
 
                 @pl.when(jnp.logical_and(has_right, index <= row))
                 def _():
@@ -294,6 +352,16 @@
                 @pl.when(jnp.logical_and(has_left, index >= row))
                 def _():
                     to_left(kind, owner, half).wait_send()
+
+    for kind in range(2):
+
+        @pl.when(has_right)
+        def _():
+            to_right(kind, first_side, 1 - mine).wait_send()
+
+        @pl.when(has_left)
+        def _():
+            to_left(kind, last_side, 1 - mine).wait_send()
 
     for tick in range(ticks):
         for strip in range(strips):
@@ -314,7 +382,7 @@
     return pl.pallas_call(
         lambda *refs: fused_kernel(n_pipe, n_head, *refs),
         out_shape=jax.ShapeDtypeStruct(queries.shape, queries.dtype),
-        in_specs=[pl.BlockSpec(memory_space=pltpu.SMEM), anywhere, anywhere, anywhere],
+        in_specs=[anywhere] * 4,
         out_specs=anywhere,
         scratch_shapes=[
             pltpu.VMEM(shape, keys.dtype),
@@ -323,6 +391,8 @@
             pltpu.VMEM(queries.shape, queries.dtype),
             pltpu.VMEM((slots, rows, HEAD_SIZE), jnp.float32),
             pltpu.VMEM((slots, rows, 2 * HEAD_SIZE), jnp.float32),
+            pltpu.SMEM(slice_index.shape, slice_index.dtype),
+            dma,
             dma((2,)),
             dma((2, 2, n_head // 2)),
             dma((2, 2, n_head // 2)),

time: 42.5 us -> 41.9 us (0.986)
  Pallas kernels: 39.2 us -> 38.6 us
    pallas_call x1, Pallas kernels: 39.2 us -> 38.6 us  [on_device(): pl.pallas_call(lambda *refs: fused_kernel(n_pipe, n_head, *refs), out_sha...]
where the time goes in v2:
time: 41.9 us; the launch traced here: 41.7 us
  Pallas kernels  38.6 us (92%)
  local copies, waits for them, and re-layouts  3.16 us (8%)
    pallas_call x1, Pallas kernels, on_device(): pl.pallas_call(lambda *refs: fused_kernel(n_pipe, n_head, *refs), out_sha...  38.6 us
    unnamed x1, local copies, waits for them, and re-layouts  3.16 us

profile of v2, /device:TPU:0, one launch (start us, length us, event | category | flops | bytes accessed | tf_op | source)
XLA Modules:
  0.0 41.7 jit_solution(9977910454934256581)
XLA Ops:
  0.0 38.6 %fused.1 = bf16[2,256,2048]{2,1,0:T(8,128)(2,1)} custom-call(s32[2,8]{1,0:T(2,128)} %refs_0_.1, bf16[2,256,2048]{2,1,0:T(8,128)(2,1)} %refs_1_.1, bf16[64,1024]{1,0:T(8,128)(2,1)} %refs_2_.1, bf16[64,1024]{1,0:T(8,128)(2,1)} %refs_3_.1), custom_call_target="tpu_custom_call" | custom-call | tf_op jit(solution)/shard_map/fused/pallas_call | solution.py:382
  38.6 3.2 %copy.6 = bf16[2,256,2048]{2,1,0:T(8,128)(2,1)} copy(bf16[2,256,2048]{2,1,0:T(8,128)(2,1)} %fused.1) | data formatting | bytes 4194304

commit v3 on v2

--- a/solution.py
+++ b/solution.py
@@ -28,8 +28,91 @@
     return jnp.concatenate([array] * count, axis=1)
 
 
-def fused_kernel(n_pipe, n_head, slice_ref, q_ref, k_ref, v_ref, o_ref, kbuf, vbuf, qbuf, obuf, best_ref, accum_ref,
-                 index_ref, index_sem, local_sem, head_send, head_recv, left_send, right_send, side_send, chunk_recv, q_sem, out_sem):
+def nearest(row, line, place):
+    reach = jnp.minimum(row, line - 1 - row)
+    offset = lax.div(place + 1, 2)
+    near = jnp.where(lax.rem(place, 2) == 1, row - offset, row + offset)
+    far = jnp.where(row < line - 1 - row, place, line - 1 - place)
+    return jnp.where(place <= 2 * reach, near, far)
+
+
+def attend(tick, start, chunks, rows, first, qbuf, kbuf, vbuf, best_ref, accum_ref, finish):
+    spans = [pl.ds(pl.multiple_of(owner * rows, rows), rows) for owner in chunks]
+    heads = qbuf.shape[2] // HEAD_SIZE
+    group = heads // (kbuf.shape[1] // HEAD_SIZE)
+    diff = lax.broadcasted_iota(jnp.int32, (rows, rows), 1) - lax.broadcasted_iota(jnp.int32, (rows, rows), 0)
+
+    limits = wide_join([jnp.where(diff <= start - owner * rows, -NEG, NEG) for owner in chunks], 1)
+
+    def score(h):
+        at = pl.ds(h * HEAD_SIZE, HEAD_SIZE)
+        kv = pl.ds(h // group * HEAD_SIZE, HEAD_SIZE)
+        query = qbuf[tick, :, at]
+        scores = wide_join([scores_of(query, kbuf[span, kv]) for span in spans], 1)
+        return jnp.minimum(scores, limits)
+
+    def rest(h, scores):
+        kv = pl.ds(h // group * HEAD_SIZE, HEAD_SIZE)
+        slot = tick * heads + h
+        top = jnp.broadcast_to(jnp.max(scores, axis=-1, keepdims=True), (rows, HEAD_SIZE))
+        if first:
+            peak = top
+        else:
+            before = best_ref[slot]
+            peak = jnp.maximum(before, top)
+        block = wide_join([vbuf[span, kv] for span in spans], 0)
+        result = weigh(scores, wide(peak, len(chunks) * rows // HEAD_SIZE), block)
+        if not first:
+            result = result + accum_ref[slot] * wide(jnp.exp2((before - peak) * TO_EXP2), 2)
+        if finish is not None:
+            finish(h, result)
+        else:
+            best_ref[slot] = peak
+            accum_ref[slot] = result
+
+    scores = score(0)
+    for h in range(heads):
+        later = score(h + 1) if h + 1 < heads else None
+        rest(h, scores)
+        scores = later
+
+
+def finish_kernel(n_pipe, index_ref, kbuf, vbuf, qbuf, best_ref, accum_ref, o_ref, obuf, out_sem):
+    me = lax.axis_index("pipe")
+    row, line = lax.div(me, 2), n_pipe // 2
+    ticks, rows, q_width = qbuf.shape
+    heads = q_width // HEAD_SIZE
+    owner = 2 * nearest(row, line, line - 1) + 1 - lax.rem(me, 2)
+
+    def strip_out(tick, strip):
+        at = pl.ds(strip * STRIP * HEAD_SIZE, STRIP * HEAD_SIZE)
+        return pltpu.make_async_copy(obuf.at[tick, :, at], o_ref.at[tick, :, at], out_sem.at[tick, strip])
+
+    @pl.loop(0, ticks)
+    def _(tick):
+        def finish(h, result):
+            obuf[tick, :, pl.ds(h * HEAD_SIZE, HEAD_SIZE)] = (result[:, :HEAD_SIZE] / result[:, HEAD_SIZE:]).astype(obuf.dtype)
+            if h % STRIP == STRIP - 1:
+                strip_out(tick, h // STRIP).start()
+
+        slice_at = index_ref[tick, me]
+
+        @pl.when(owner <= slice_at)
+        def _():
+            attend(tick, slice_at * rows, [owner], rows, False, qbuf, kbuf, vbuf, best_ref, accum_ref, finish)
+
+        @pl.when(owner > slice_at)
+        def _():
+            for h in range(heads):
+                finish(h, accum_ref[tick * heads + h])
+
+    for tick in range(ticks):
+        for strip in range(heads // STRIP):
+            strip_out(tick, strip).wait()
+
+
+def gather_kernel(n_pipe, n_head, slice_ref, q_ref, k_ref, v_ref, kbuf, vbuf, qbuf, best_ref, accum_ref,
+                  index_ref, index_sem, local_sem, head_send, head_recv, left_send, right_send, side_send, chunk_recv, q_sem):
     me = lax.axis_index("pipe")
     head = lax.axis_index("head")
     side = me + 1 - 2 * lax.rem(me, 2)
@@ -221,64 +304,20 @@
                 def _():
                     to_left(kind, last_side, 1 - mine).start()
 
-    ticks, _, q_width = qbuf.shape
-    heads = q_width // HEAD_SIZE
-    kv_heads = width // HEAD_SIZE
-    group = heads // kv_heads
-    diff = lax.broadcasted_iota(jnp.int32, (rows, rows), 1) - lax.broadcasted_iota(jnp.int32, (rows, rows), 0)
-    reach = jnp.minimum(row, line - 1 - row)
-
-    def nearest(place):
-        offset = lax.div(place + 1, 2)
-        near = jnp.where(lax.rem(place, 2) == 1, row - offset, row + offset)
-        far = jnp.where(row < line - 1 - row, place, line - 1 - place)
-        return jnp.where(place <= 2 * reach, near, far)
-
-    strips = heads // STRIP
-
-    def strip_out(tick, strip):
-        at = pl.ds(strip * STRIP * HEAD_SIZE, STRIP * HEAD_SIZE)
-        return pltpu.make_async_copy(obuf.at[tick, :, at], o_ref.at[tick, :, at], out_sem.at[tick, strip])
-
-    def compute(chunks, first, last, before_tick):
-        spans = [pl.ds(pl.multiple_of(owner * rows, rows), rows) for owner in chunks]
-
+    ticks = qbuf.shape[0]
+
+    def compute(chunks, first, before_tick):
         @pl.loop(0, ticks)
         def _(tick):
             before_tick(tick)
             start = index_ref[tick, me] * rows
-            for h in range(heads):
-                at = pl.ds(h * HEAD_SIZE, HEAD_SIZE)
-                kv = pl.ds(h // group * HEAD_SIZE, HEAD_SIZE)
-                slot = tick * heads + h
-                query = qbuf[tick, :, at]
-                scores = wide_join([
-                    jnp.where(diff <= start - owner * rows, scores_of(query, kbuf[span, kv]), NEG)
-                    for owner, span in zip(chunks, spans)
-                ], 1)
-                top = jnp.broadcast_to(jnp.max(scores, axis=-1, keepdims=True), (rows, HEAD_SIZE))
-                if first:
-                    peak = top
-                else:
-                    before = best_ref[slot]
-                    peak = jnp.maximum(before, top)
-                block = wide_join([vbuf[span, kv] for span in spans], 0)
-                result = weigh(scores, wide(peak, len(chunks) * rows // HEAD_SIZE), block)
-                if not first:
-                    result = result + accum_ref[slot] * wide(jnp.exp2((before - peak) * TO_EXP2), 2)
-                if last:
-                    obuf[tick, :, at] = (result[:, :HEAD_SIZE] / result[:, HEAD_SIZE:]).astype(obuf.dtype)
-                    if h % STRIP == STRIP - 1:
-                        strip_out(tick, h // STRIP).start()
-                else:
-                    best_ref[slot] = peak
-                    accum_ref[slot] = result
+            attend(tick, start, chunks, rows, first, qbuf, kbuf, vbuf, best_ref, accum_ref, None)
 
     def side_owner(place):
-        return 2 * nearest(place) + lax.rem(side, 2)
+        return 2 * nearest(row, line, place) + lax.rem(side, 2)
 
     def own_owner(place):
-        return 2 * nearest(place) + lax.rem(me, 2)
+        return 2 * nearest(row, line, place) + lax.rem(me, 2)
 
     def side_wait(owner):
         for order in range(2):
@@ -296,7 +335,7 @@
     relay_at = first_events
     pltpu.make_async_copy(slice_ref, index_ref, index_sem).wait()
     pltpu.make_async_copy(q_ref, qbuf, q_sem).wait()
-    compute([me], True, False, relay_at)
+    compute([me], True, relay_at)
 
     @pl.loop(1, line)
     def _(step):
@@ -318,15 +357,10 @@
             def _():
                 relay(step + 1, 0)
 
-        compute([own_owner(step), side_owner(step - 1)], False, False, events)
-
-    def last_events(tick):
-        @pl.when(tick == 0)
-        def _():
-            side_wait(side_owner(line - 1))
-            guests_pass(line - 1)
-
-    compute([side_owner(line - 1)], False, True, last_events)
+        compute([own_owner(step), side_owner(step - 1)], False, events)
+
+    side_wait(side_owner(line - 1))
+    guests_pass(line - 1)
 
     for kind in range(2):
         for shift in range(1, near_heads):
@@ -363,10 +397,6 @@
         def _():
             to_left(kind, last_side, 1 - mine).wait_send()
 
-    for tick in range(ticks):
-        for strip in range(strips):
-            strip_out(tick, strip).wait()
-
 
 def wide_join(parts, axis):
     return parts[0] if len(parts) == 1 else jnp.concatenate(parts, axis=axis)
@@ -377,20 +407,21 @@
     ticks, rows, columns = queries.shape
     shape = (rows * n_pipe, keys.shape[1] // n_head)
     slots = ticks * columns // HEAD_SIZE
-    anywhere = pl.BlockSpec(memory_space=pl.ANY)
+    anywhere = pl.BlockSpec(memory_space=pltpu.HBM)
     dma = pltpu.SemaphoreType.DMA
-    return pl.pallas_call(
-        lambda *refs: fused_kernel(n_pipe, n_head, *refs),
-        out_shape=jax.ShapeDtypeStruct(queries.shape, queries.dtype),
-        in_specs=[anywhere] * 4,
-        out_specs=anywhere,
-        scratch_shapes=[
+    fast = pl.BlockSpec(memory_space=pltpu.VMEM)
+    state = pl.pallas_call(
+        lambda *refs: gather_kernel(n_pipe, n_head, *refs),
+        out_shape=[
             pltpu.VMEM(shape, keys.dtype),
             pltpu.VMEM(shape, keys.dtype),
             pltpu.VMEM(queries.shape, queries.dtype),
-            pltpu.VMEM(queries.shape, queries.dtype),
             pltpu.VMEM((slots, rows, HEAD_SIZE), jnp.float32),
             pltpu.VMEM((slots, rows, 2 * HEAD_SIZE), jnp.float32),
+        ],
+        in_specs=[anywhere] * 4,
+        out_specs=[fast] * 5,
+        scratch_shapes=[
             pltpu.SMEM(slice_index.shape, slice_index.dtype),
             dma,
             dma((2,)),
@@ -401,11 +432,22 @@
             dma((2, n_pipe, 2)),
             dma((2, n_pipe, 2)),
             dma,
+        ],
+        compiler_params=pltpu.CompilerParams(collective_id=0, has_side_effects=True, vmem_limit_bytes=30 * 2 ** 20),
+        name="gather",
+    )(*(pltpu.with_memory_space_constraint(array, pltpu.HBM) for array in (slice_index, queries, keys, values)))
+    return pl.pallas_call(
+        lambda *refs: finish_kernel(n_pipe, *refs),
+        out_shape=jax.ShapeDtypeStruct(queries.shape, queries.dtype),
+        in_specs=[pl.BlockSpec(memory_space=pltpu.SMEM)] + [fast] * 5,
+        out_specs=anywhere,
+        scratch_shapes=[
+            pltpu.VMEM(queries.shape, queries.dtype),
             dma((ticks, columns // HEAD_SIZE // STRIP)),
         ],
-        compiler_params=pltpu.CompilerParams(collective_id=0, has_side_effects=True, vmem_limit_bytes=60 * 2 ** 20),
-        name="fused",
-    )(slice_index, queries, keys, values)
+        compiler_params=pltpu.CompilerParams(vmem_limit_bytes=30 * 2 ** 20),
+        name="finish",
+    )(slice_index, *state)
 
 
 def solution(mesh):

time: 41.9 us -> 39.5 us (0.943)
  the two profiles are of different devices: /device:TPU:0 before, /device:TPU:19 now
where the time goes in v3:
time: 39.5 us; the launch traced here: 38.7 us
  Pallas kernels  38.7 us (98%)
    pallas_call x1, Pallas kernels, on_device(): pl.pallas_call(lambda *refs: gather_kernel(n_pipe, n_head, *refs), out_sh...  32.5 us
    pallas_call x1, Pallas kernels, on_device(): pl.pallas_call(lambda *refs: finish_kernel(n_pipe, *refs), out_shape=jax....  6.13 us

profile of v3, /device:TPU:19, one launch (start us, length us, event | category | flops | bytes accessed | tf_op | source)
XLA Modules:
  0.0 38.7 jit_solution(7637326466521188803)
XLA Ops:
  0.0 0.0 copy-start
  0.0 32.5 %gather.1 = (bf16[2048,256]{1,0:T(8,128)(2,1)S(1)}, bf16[2048,256]{1,0:T(8,128)(2,1)S(1)}, bf16[2,256,2048]{2,1,0:T(8,128)(2,1)S(1)}, f32[32,256,128]{2,1,0:T(8,128)S(1)}, f32[32,256,256]{2,1,0:T(8,128)S(1)}) custom-call(s32[2,8]{1,0:T(2,128)} %refs_0_.3, bf16[2,256,2048]{2,1,0:T(8,128)(2,1)} %refs_1_.1, bf16[64,1024]{1,0:T(8,128)(2,1)} %refs_2_.1, ...), custom_call_target="tpu_custom_call" | custom-call | tf_op jit(solution)/shard_map/gather/pallas_call | solution.py:413
  32.5 0.0 copy-done
  32.6 6.1 %finish.1 = bf16[2,256,2048]{2,1,0:T(8,128)(2,1)} custom-call(s32[2,8]{1,0:T(2,128)S(1)} %copy-done, bf16[2048,256]{1,0:T(8,128)(2,1)S(1)} %get-tuple-element.10.refs_1_, bf16[2048,256]{1,0:T(8,128)(2,1)S(1)} %get-tuple-element.11.refs_2_, bf16[2,256,2048]{2,1,0:T(8,128)(2,1)S(1)} %get-tuple-element.12.refs_3_, ...), custom_call_target="tpu_custom_call" | custom-call | tf_op jit(solution)/shard_map/finish/pallas_call | solution.py:439
Async XLA Ops:
  0.0 32.5 %copy-start = (s32[2,8]{1,0:T(2,128)S(1)}, s32[2,8]{1,0:T(2,128)}, u32[]{:S(2)}) copy-start(s32[2,8]{1,0:T(2,128)} %refs_0_.3) | copy-start | bytes 196

commit v4 on v3

--- a/solution.py
+++ b/solution.py
@@ -11,7 +11,7 @@
 NEG = -1e30
 TO_EXP2 = HEAD_SIZE ** (-0.5) * math.log2(math.e)
 MESH = pl.DeviceIdType.MESH
-STRIP = 4
+STRIP = 16
 
 
 def scores_of(query, key_block):
@@ -36,20 +36,19 @@
     return jnp.where(place <= 2 * reach, near, far)
 
 
-def attend(tick, start, chunks, rows, first, qbuf, kbuf, vbuf, best_ref, accum_ref, finish):
-    spans = [pl.ds(pl.multiple_of(owner * rows, rows), rows) for owner in chunks]
+def attend(tick, start, firsts, rows, first, qbuf, kbuf, vbuf, best_ref, accum_ref, finish):
+    half = rows // 2
+    spans = [pl.ds(pl.multiple_of(at, half), half) for at in firsts]
     heads = qbuf.shape[2] // HEAD_SIZE
     group = heads // (kbuf.shape[1] // HEAD_SIZE)
-    diff = lax.broadcasted_iota(jnp.int32, (rows, rows), 1) - lax.broadcasted_iota(jnp.int32, (rows, rows), 0)
-
-    limits = wide_join([jnp.where(diff <= start - owner * rows, -NEG, NEG) for owner in chunks], 1)
+    diff = lax.broadcasted_iota(jnp.int32, (rows, half), 1) - lax.broadcasted_iota(jnp.int32, (rows, half), 0)
+    limits = wide_join([jnp.where(diff <= start - at, -NEG, NEG) for at in firsts], 1)
 
     def score(h):
         at = pl.ds(h * HEAD_SIZE, HEAD_SIZE)
         kv = pl.ds(h // group * HEAD_SIZE, HEAD_SIZE)
-        query = qbuf[tick, :, at]
-        scores = wide_join([scores_of(query, kbuf[span, kv]) for span in spans], 1)
-        return jnp.minimum(scores, limits)
+        block = wide_join([kbuf[span, kv] for span in spans], 0)
+        return jnp.minimum(scores_of(qbuf[tick, :, at], block), limits)
 
     def rest(h, scores):
         kv = pl.ds(h // group * HEAD_SIZE, HEAD_SIZE)
@@ -61,7 +60,7 @@
             before = best_ref[slot]
             peak = jnp.maximum(before, top)
         block = wide_join([vbuf[span, kv] for span in spans], 0)
-        result = weigh(scores, wide(peak, len(chunks) * rows // HEAD_SIZE), block)
+        result = weigh(scores, wide(peak, len(firsts) * half // HEAD_SIZE), block)
         if not first:
             result = result + accum_ref[slot] * wide(jnp.exp2((before - peak) * TO_EXP2), 2)
         if finish is not None:
@@ -77,12 +76,18 @@
         scores = later
 
 
-def finish_kernel(n_pipe, index_ref, kbuf, vbuf, qbuf, best_ref, accum_ref, o_ref, obuf, out_sem):
+def finish_kernel(n_pipe, n_head, index_ref, kbuf, vbuf, qbuf, best_ref, accum_ref, o_ref, obuf, out_sem):
     me = lax.axis_index("pipe")
     row, line = lax.div(me, 2), n_pipe // 2
     ticks, rows, q_width = qbuf.shape
     heads = q_width // HEAD_SIZE
-    owner = 2 * nearest(row, line, line - 1) + 1 - lax.rem(me, 2)
+    mine = lax.div(lax.axis_index("head"), n_head // 2)
+    half = rows // 2
+    own_base = (2 * nearest(row, line, line - 1) + lax.rem(me, 2)) * rows
+    side_base = (2 * nearest(row, line, line - 2) + 1 - lax.rem(me, 2)) * rows
+    last_base = (2 * nearest(row, line, line - 1) + 1 - lax.rem(me, 2)) * rows
+    firsts = [own_base + (1 - mine) * half, side_base + (1 - mine) * half, last_base, last_base + half]
+    least = jnp.minimum(jnp.minimum(firsts[0], firsts[1]), last_base)
 
     def strip_out(tick, strip):
         at = pl.ds(strip * STRIP * HEAD_SIZE, STRIP * HEAD_SIZE)
@@ -91,17 +96,17 @@
     @pl.loop(0, ticks)
     def _(tick):
         def finish(h, result):
-            obuf[tick, :, pl.ds(h * HEAD_SIZE, HEAD_SIZE)] = (result[:, :HEAD_SIZE] / result[:, HEAD_SIZE:]).astype(obuf.dtype)
+            obuf[tick, :, pl.ds(h * HEAD_SIZE, HEAD_SIZE)] = (result[:, :HEAD_SIZE] * pl.reciprocal(result[:, HEAD_SIZE:])).astype(obuf.dtype)
             if h % STRIP == STRIP - 1:
                 strip_out(tick, h // STRIP).start()
 
-        slice_at = index_ref[tick, me]
-
-        @pl.when(owner <= slice_at)
-        def _():
-            attend(tick, slice_at * rows, [owner], rows, False, qbuf, kbuf, vbuf, best_ref, accum_ref, finish)
-
-        @pl.when(owner > slice_at)
+        start = index_ref[tick, me] * rows
+
+        @pl.when(least < start + rows)
+        def _():
+            attend(tick, start, firsts, rows, False, qbuf, kbuf, vbuf, best_ref, accum_ref, finish)
+
+        @pl.when(least >= start + rows)
         def _():
             for h in range(heads):
                 finish(h, accum_ref[tick * heads + h])
@@ -111,8 +116,8 @@
             strip_out(tick, strip).wait()
 
 
-def gather_kernel(n_pipe, n_head, slice_ref, q_ref, k_ref, v_ref, kbuf, vbuf, qbuf, best_ref, accum_ref,
-                  index_ref, index_sem, local_sem, head_send, head_recv, left_send, right_send, side_send, chunk_recv, q_sem):
+def gather_kernel(n_pipe, n_head, slice_ref, q_ref, k_ref, v_ref, kbuf, vbuf, qbuf, best_ref, accum_ref, index_ref,
+                  index_sem, local_sem, head_send, head_recv, left_send, right_send, side_send, chunk_recv, q_sem):
     me = lax.axis_index("pipe")
     head = lax.axis_index("head")
     side = me + 1 - 2 * lax.rem(me, 2)
@@ -285,6 +290,12 @@
             def _():
                 to_left(kind, last_side, 1 - mine).start()
 
+    def guests(step):
+        if isinstance(step, int):
+            guests_start()
+        else:
+            guests_pass(step - 1)
+
     def guests_pass(distance):
         for kind in range(2):
 
@@ -306,12 +317,12 @@
 
     ticks = qbuf.shape[0]
 
-    def compute(chunks, first, before_tick):
+    def compute(firsts, first, before_tick):
         @pl.loop(0, ticks)
         def _(tick):
             before_tick(tick)
             start = index_ref[tick, me] * rows
-            attend(tick, start, chunks, rows, first, qbuf, kbuf, vbuf, best_ref, accum_ref, None)
+            attend(tick, start, firsts, rows, first, qbuf, kbuf, vbuf, best_ref, accum_ref, None)
 
     def side_owner(place):
         return 2 * nearest(row, line, place) + lax.rem(side, 2)
@@ -319,47 +330,44 @@
     def own_owner(place):
         return 2 * nearest(row, line, place) + lax.rem(me, 2)
 
-    def side_wait(owner):
-        for order in range(2):
-
-            @pl.when(crosses(lax.div(owner, 2), order))
-            def _():
-                for kind in range(2):
-                    to_side(kind, owner, halves(order)).wait_recv()
-
-    def first_events(tick):
-        @pl.when(tick == 0)
-        def _():
-            relay(1, 0)
-
-    relay_at = first_events
+    def side_wait(place, order):
+        owner = side_owner(place)
+
+        @pl.when(crosses(lax.div(owner, 2), order))
+        def _():
+            for kind in range(2):
+                to_side(kind, owner, halves(order)).wait_recv()
+
+    def part(owner, order):
+        return owner * rows + halves(order) * half_rows
+
+    def events(step):
+        def before(tick):
+            @pl.when(tick == 0)
+            def _():
+                relay(step, 0)
+                side_wait(step - 1, 0)
+
+            @pl.when(tick == 1)
+            def _():
+                relay(step, 1)
+                side_wait(step - 1, 1)
+                guests(step)
+
+        return before
+
     pltpu.make_async_copy(slice_ref, index_ref, index_sem).wait()
     pltpu.make_async_copy(q_ref, qbuf, q_sem).wait()
-    compute([me], True, relay_at)
-
-    @pl.loop(1, line)
+    compute([part(me, 0), part(me, 1), part(own_owner(1), 0), part(side_owner(0), 0)], True, events(1))
+
+    @pl.loop(2, line)
     def _(step):
-        def events(tick):
-            @pl.when(tick == 0)
-            def _():
-                relay(step, 1)
-                side_wait(side_owner(step - 1))
-
-                @pl.when(step == 1)
-                def _():
-                    guests_start()
-
-                @pl.when(step > 1)
-                def _():
-                    guests_pass(step - 1)
-
-            @pl.when(tick == 1)
-            def _():
-                relay(step + 1, 0)
-
-        compute([own_owner(step), side_owner(step - 1)], False, events)
-
-    side_wait(side_owner(line - 1))
+        compute([
+            part(own_owner(step - 1), 1), part(side_owner(step - 2), 1), part(own_owner(step), 0), part(side_owner(step - 1), 0)
+        ], False, events(step))
+
+    for order in range(2):
+        side_wait(line - 1, order)
     guests_pass(line - 1)
 
     for kind in range(2):
@@ -418,11 +426,11 @@
             pltpu.VMEM(queries.shape, queries.dtype),
             pltpu.VMEM((slots, rows, HEAD_SIZE), jnp.float32),
             pltpu.VMEM((slots, rows, 2 * HEAD_SIZE), jnp.float32),
+            pltpu.SMEM(slice_index.shape, slice_index.dtype),
         ],
         in_specs=[anywhere] * 4,
-        out_specs=[fast] * 5,
+        out_specs=[fast] * 5 + [pl.BlockSpec(memory_space=pltpu.SMEM)],
         scratch_shapes=[
-            pltpu.SMEM(slice_index.shape, slice_index.dtype),
             dma,
             dma((2,)),
             dma((2, 2, n_head // 2)),
@@ -437,7 +445,7 @@
         name="gather",
     )(*(pltpu.with_memory_space_constraint(array, pltpu.HBM) for array in (slice_index, queries, keys, values)))
     return pl.pallas_call(
-        lambda *refs: finish_kernel(n_pipe, *refs),
+        lambda *refs: finish_kernel(n_pipe, n_head, *refs),
         out_shape=jax.ShapeDtypeStruct(queries.shape, queries.dtype),
         in_specs=[pl.BlockSpec(memory_space=pltpu.SMEM)] + [fast] * 5,
         out_specs=anywhere,
@@ -447,7 +455,7 @@
         ],
         compiler_params=pltpu.CompilerParams(vmem_limit_bytes=30 * 2 ** 20),
         name="finish",
-    )(slice_index, *state)
+    )(state[5], *state[:5])
 
 
 def solution(mesh):

time: 39.5 us -> 35.7 us (0.904)
  the two profiles are of different devices: /device:TPU:19 before, /device:TPU:27 now
where the time goes in v4:
time: 35.7 us; the launch traced here: 35.5 us
  Pallas kernels  35.5 us (99%)
    pallas_call x1, Pallas kernels, on_device(): pl.pallas_call(lambda *refs: gather_kernel(n_pipe, n_head, *refs), out_sh...  28 us
    pallas_call x1, Pallas kernels, on_device(): pl.pallas_call(lambda *refs: finish_kernel(n_pipe, n_head, *refs), out_sh...  7.48 us

profile of v4, /device:TPU:27, one launch (start us, length us, event | category | flops | bytes accessed | tf_op | source)
XLA Modules:
  0.0 35.5 jit_solution(2920879688492453236)
XLA Ops:
  0.0 28.0 %gather.1 = (bf16[2048,256]{1,0:T(8,128)(2,1)S(1)}, bf16[2048,256]{1,0:T(8,128)(2,1)S(1)}, bf16[2,256,2048]{2,1,0:T(8,128)(2,1)S(1)}, f32[32,256,128]{2,1,0:T(8,...) custom-call(s32[2,8]{1,0:T(2,128)} %refs_0_.1, bf16[2,256,2048]{2,1,0:T(8,128)(2,1)} %refs_1_.1, ...), custom_call_target="tpu_custom_call" | custom-call | tf_op jit(solution)/shard_map/gather/pallas_call | solution.py:421
  28.1 7.5 %finish.1 = bf16[2,256,2048]{2,1,0:T(8,128)(2,1)} custom-call(s32[2,8]{1,0:T(2,128)S(4)} %get-tuple-element.11.refs_0_, bf16[2048,256]{1,0:T(8,128)(2,1)S(1)} %get-tuple-element.12.refs_1_, bf16[2048,256]{1,0:T(8,128)(2,1)S(1)} %get-tuple-element.13.refs_2_, bf16[2,256,2048]{2,1,0:T(8,128)(2,1)S(1)} %get-tuple-element.14.refs_3_, ...), custom_call_target="tpu_custom_call" | custom-call | tf_op jit(solution)/shard_map/finish/pallas_call | solution.py:447

commit v5 on v4

--- a/solution.py
+++ b/solution.py
@@ -11,7 +11,7 @@
 NEG = -1e30
 TO_EXP2 = HEAD_SIZE ** (-0.5) * math.log2(math.e)
 MESH = pl.DeviceIdType.MESH
-STRIP = 16
+STRIP = 4
 
 
 def scores_of(query, key_block):
@@ -36,7 +36,7 @@
     return jnp.where(place <= 2 * reach, near, far)
 
 
-def attend(tick, start, firsts, rows, first, qbuf, kbuf, vbuf, best_ref, accum_ref, finish):
+def attend(tick, start, firsts, rows, qbuf, kbuf, vbuf, best_ref, accum_ref, finish):
     half = rows // 2
     spans = [pl.ds(pl.multiple_of(at, half), half) for at in firsts]
     heads = qbuf.shape[2] // HEAD_SIZE
@@ -54,15 +54,11 @@
         kv = pl.ds(h // group * HEAD_SIZE, HEAD_SIZE)
         slot = tick * heads + h
         top = jnp.broadcast_to(jnp.max(scores, axis=-1, keepdims=True), (rows, HEAD_SIZE))
-        if first:
-            peak = top
-        else:
-            before = best_ref[slot]
-            peak = jnp.maximum(before, top)
+        before = best_ref[slot]
+        peak = jnp.maximum(before, top)
         block = wide_join([vbuf[span, kv] for span in spans], 0)
         result = weigh(scores, wide(peak, len(firsts) * half // HEAD_SIZE), block)
-        if not first:
-            result = result + accum_ref[slot] * wide(jnp.exp2((before - peak) * TO_EXP2), 2)
+        result = result + accum_ref[slot] * wide(jnp.exp2((before - peak) * TO_EXP2), 2)
         if finish is not None:
             finish(h, result)
         else:
@@ -104,7 +100,7 @@
 
         @pl.when(least < start + rows)
         def _():
-            attend(tick, start, firsts, rows, False, qbuf, kbuf, vbuf, best_ref, accum_ref, finish)
+            attend(tick, start, firsts, rows, qbuf, kbuf, vbuf, best_ref, accum_ref, finish)
 
         @pl.when(least >= start + rows)
         def _():
@@ -158,6 +154,11 @@
         keep(kind).start()
     pltpu.make_async_copy(slice_ref, index_ref, index_sem).start()
     pltpu.make_async_copy(q_ref, qbuf, q_sem).start()
+    @pl.loop(0, best_ref.shape[0])
+    def _(slot):
+        best_ref[slot] = jnp.full(best_ref.shape[1:], NEG, best_ref.dtype)
+        accum_ref[slot] = jnp.zeros(accum_ref.shape[1:], accum_ref.dtype)
+
     pl.semaphore_wait(barrier, n_head + jnp.where(has_left, 1, 0) + jnp.where(has_right, 1, 0))
 
     def chunk(kind, owner, half):
@@ -291,9 +292,12 @@
                 to_left(kind, last_side, 1 - mine).start()
 
     def guests(step):
-        if isinstance(step, int):
+        @pl.when(step == 1)
+        def _():
             guests_start()
-        else:
+
+        @pl.when(step > 1)
+        def _():
             guests_pass(step - 1)
 
     def guests_pass(distance):
@@ -317,12 +321,12 @@
 
     ticks = qbuf.shape[0]
 
-    def compute(firsts, first, before_tick):
+    def compute(firsts, before_tick):
         @pl.loop(0, ticks)
         def _(tick):
             before_tick(tick)
             start = index_ref[tick, me] * rows
-            attend(tick, start, firsts, rows, first, qbuf, kbuf, vbuf, best_ref, accum_ref, None)
+            attend(tick, start, firsts, rows, qbuf, kbuf, vbuf, best_ref, accum_ref, None)
 
     def side_owner(place):
         return 2 * nearest(row, line, place) + lax.rem(side, 2)
@@ -358,13 +362,10 @@
 
     pltpu.make_async_copy(slice_ref, index_ref, index_sem).wait()
     pltpu.make_async_copy(q_ref, qbuf, q_sem).wait()
-    compute([part(me, 0), part(me, 1), part(own_owner(1), 0), part(side_owner(0), 0)], True, events(1))
-
-    @pl.loop(2, line)
+    @pl.loop(1, line)
     def _(step):
-        compute([
-            part(own_owner(step - 1), 1), part(side_owner(step - 2), 1), part(own_owner(step), 0), part(side_owner(step - 1), 0)
-        ], False, events(step))
+        older = jnp.where(step == 1, part(me, 0), part(side_owner(step - 2), 1))
+        compute([part(own_owner(step - 1), 1), older, part(own_owner(step), 0), part(side_owner(step - 1), 0)], events(step))
 
     for order in range(2):
         side_wait(line - 1, order)

time: 35.7 us -> 35.2 us (0.986)
  the two profiles are of different devices: /device:TPU:27 before, /device:TPU:0 now
where the time goes in v5:
time: 35.2 us; the launch traced here: 34.8 us
  Pallas kernels  34.8 us (99%)
    pallas_call x1, Pallas kernels, on_device(): pl.pallas_call(lambda *refs: gather_kernel(n_pipe, n_head, *refs), out_sh...  30.4 us
    pallas_call x1, Pallas kernels, on_device(): pl.pallas_call(lambda *refs: finish_kernel(n_pipe, n_head, *refs), out_sh...  4.4 us

profile of v5, /device:TPU:0, one launch (start us, length us, event | category | flops | bytes accessed | tf_op | source)
XLA Modules:
  0.0 34.8 jit_solution(827458396560553859)
XLA Ops:
  0.0 30.4 %gather.1 = (bf16[2048,256]{1,0:T(8,128)(2,1)S(1)}, bf16[2048,256]{1,0:T(8,128)(2,1)S(1)}, bf16[2,256,2048]{2,1,0:T(8,128)(2,1)S(1)}, f32[32,256,128]{2,1,0:T(8,...) custom-call(s32[2,8]{1,0:T(2,128)} %refs_0_.1, bf16[2,256,2048]{2,1,0:T(8,128)(2,1)} %refs_1_.1, ...), custom_call_target="tpu_custom_call" | custom-call | tf_op jit(solution)/shard_map/gather/pallas_call | solution.py:422
  30.4 4.4 %finish.1 = bf16[2,256,2048]{2,1,0:T(8,128)(2,1)} custom-call(s32[2,8]{1,0:T(2,128)S(4)} %get-tuple-element.11.refs_0_, bf16[2048,256]{1,0:T(8,128)(2,1)S(1)} %get-tuple-element.12.refs_1_, bf16[2048,256]{1,0:T(8,128)(2,1)S(1)} %get-tuple-element.13.refs_2_, bf16[2,256,2048]{2,1,0:T(8,128)(2,1)S(1)} %get-tuple-element.14.refs_3_, ...), custom_call_target="tpu_custom_call" | custom-call | tf_op jit(solution)/shard_map/finish/pallas_call | solution.py:448

commit v6 on v5

--- a/solution.py
+++ b/solution.py
@@ -98,9 +98,15 @@
 
         start = index_ref[tick, me] * rows
 
-        @pl.when(least < start + rows)
+        sees_last = last_base < start + rows
+
+        @pl.when(sees_last)
         def _():
             attend(tick, start, firsts, rows, qbuf, kbuf, vbuf, best_ref, accum_ref, finish)
+
+        @pl.when(jnp.logical_and(least < start + rows, jnp.logical_not(sees_last)))
+        def _():
+            attend(tick, start, firsts[:2], rows, qbuf, kbuf, vbuf, best_ref, accum_ref, finish)
 
         @pl.when(least >= start + rows)
         def _():
@@ -113,7 +119,7 @@
 
 
 def gather_kernel(n_pipe, n_head, slice_ref, q_ref, k_ref, v_ref, kbuf, vbuf, qbuf, best_ref, accum_ref, index_ref,
-                  index_sem, local_sem, head_send, head_recv, left_send, right_send, side_send, chunk_recv, q_sem):
+                  index_sem, kstage, vstage, stage_sem, local_sem, head_send, head_recv, left_send, right_send, side_send, chunk_recv, q_sem):
     me = lax.axis_index("pipe")
     head = lax.axis_index("head")
     side = me + 1 - 2 * lax.rem(me, 2)
@@ -126,7 +132,7 @@
     half_rows = rows // 2
     mine = lax.div(head, near_heads)
     width = kbuf.shape[1]
-    ins, bufs = (k_ref, v_ref), (kbuf, vbuf)
+    inputs, ins, bufs = (k_ref, v_ref), (kstage, vstage), (kbuf, vbuf)
 
     barrier = pltpu.get_barrier_semaphore()
     for other in range(1, n_head):
@@ -151,7 +157,7 @@
         return pltpu.make_async_copy(columns(kind, head), spot(kind, head), local_sem.at[kind])
 
     for kind in range(2):
-        keep(kind).start()
+        pltpu.make_async_copy(inputs[kind], ins[kind], stage_sem.at[kind]).start()
     pltpu.make_async_copy(slice_ref, index_ref, index_sem).start()
     pltpu.make_async_copy(q_ref, qbuf, q_sem).start()
     @pl.loop(0, best_ref.shape[0])
@@ -159,6 +165,9 @@
         best_ref[slot] = jnp.full(best_ref.shape[1:], NEG, best_ref.dtype)
         accum_ref[slot] = jnp.zeros(accum_ref.shape[1:], accum_ref.dtype)
 
+    for kind in range(2):
+        pltpu.make_async_copy(inputs[kind], ins[kind], stage_sem.at[kind]).wait()
+        keep(kind).start()
     pl.semaphore_wait(barrier, n_head + jnp.where(has_left, 1, 0) + jnp.where(has_right, 1, 0))
 
     def chunk(kind, owner, half):
@@ -433,6 +442,9 @@
         out_specs=[fast] * 5 + [pl.BlockSpec(memory_space=pltpu.SMEM)],
         scratch_shapes=[
             dma,
+            pltpu.VMEM(keys.shape, keys.dtype),
+            pltpu.VMEM(values.shape, values.dtype),
+            dma((2,)),
             dma((2,)),
             dma((2, 2, n_head // 2)),
             dma((2, 2, n_head // 2)),

time: 35.2 us -> 34.8 us (0.989)
  the two profiles are of different devices: /device:TPU:0 before, /device:TPU:28 now
where the time goes in v6:
time: 34.8 us; the launch traced here: 34.7 us
  Pallas kernels  34.7 us (100%)
    pallas_call x1, Pallas kernels, on_device(): pl.pallas_call(lambda *refs: gather_kernel(n_pipe, n_head, *refs), out_sh...  27.4 us
    pallas_call x1, Pallas kernels, on_device(): pl.pallas_call(lambda *refs: finish_kernel(n_pipe, n_head, *refs), out_sh...  7.28 us

profile of v6, /device:TPU:28, one launch (start us, length us, event | category | flops | bytes accessed | tf_op | source)
XLA Modules:
  0.0 34.7 jit_solution(15449764109943566037)
XLA Ops:
  0.0 27.4 %gather.1 = (bf16[2048,256]{1,0:T(8,128)(2,1)S(1)}, bf16[2048,256]{1,0:T(8,128)(2,1)S(1)}, bf16[2,256,2048]{2,1,0:T(8,128)(2,1)S(1)}, f32[32,256,128]{2,1,0:T(8,...) custom-call(s32[2,8]{1,0:T(2,128)} %refs_0_.1, bf16[2,256,2048]{2,1,0:T(8,128)(2,1)} %refs_1_.1, ...), custom_call_target="tpu_custom_call" | custom-call | tf_op jit(solution)/shard_map/gather/pallas_call | solution.py:431
  27.4 7.3 %finish.1 = bf16[2,256,2048]{2,1,0:T(8,128)(2,1)} custom-call(s32[2,8]{1,0:T(2,128)S(4)} %get-tuple-element.11.refs_0_, bf16[2048,256]{1,0:T(8,128)(2,1)S(1)} %get-tuple-element.12.refs_1_, bf16[2048,256]{1,0:T(8,128)(2,1)S(1)} %get-tuple-element.13.refs_2_, bf16[2,256,2048]{2,1,0:T(8,128)(2,1)S(1)} %get-tuple-element.14.refs_3_, ...), custom_call_target="tpu_custom_call" | custom-call | tf_op jit(solution)/shard_map/finish/pallas_call | solution.py:460

commit v7 on v6

--- a/solution.py
+++ b/solution.py
@@ -1,3 +1,4 @@
+import functools
 import math
 
 import jax
@@ -36,7 +37,7 @@
     return jnp.where(place <= 2 * reach, near, far)
 
 
-def attend(tick, start, firsts, rows, qbuf, kbuf, vbuf, best_ref, accum_ref, finish):
+def plan(tick, start, firsts, rows, qbuf, kbuf, vbuf, best_ref, accum_ref, finish):
     half = rows // 2
     spans = [pl.ds(pl.multiple_of(at, half), half) for at in firsts]
     heads = qbuf.shape[2] // HEAD_SIZE
@@ -65,11 +66,19 @@
             best_ref[slot] = peak
             accum_ref[slot] = result
 
-    scores = score(0)
-    for h in range(heads):
-        later = score(h + 1) if h + 1 < heads else None
-        rest(h, scores)
+    return [(functools.partial(score, h), functools.partial(rest, h)) for h in range(heads)]
+
+
+def follow(steps):
+    scores = steps[0][0]()
+    for at, (_, rest) in enumerate(steps):
+        later = steps[at + 1][0]() if at + 1 < len(steps) else None
+        rest(scores)
         scores = later
+
+
+def attend(*args):
+    follow(plan(*args))
 
 
 def finish_kernel(n_pipe, n_head, index_ref, kbuf, vbuf, qbuf, best_ref, accum_ref, o_ref, obuf, out_sem):
@@ -89,29 +98,41 @@
         at = pl.ds(strip * STRIP * HEAD_SIZE, STRIP * HEAD_SIZE)
         return pltpu.make_async_copy(obuf.at[tick, :, at], o_ref.at[tick, :, at], out_sem.at[tick, strip])
 
-    @pl.loop(0, ticks)
-    def _(tick):
-        def finish(h, result):
-            obuf[tick, :, pl.ds(h * HEAD_SIZE, HEAD_SIZE)] = (result[:, :HEAD_SIZE] * pl.reciprocal(result[:, HEAD_SIZE:])).astype(obuf.dtype)
-            if h % STRIP == STRIP - 1:
-                strip_out(tick, h // STRIP).start()
-
-        start = index_ref[tick, me] * rows
-
-        sees_last = last_base < start + rows
-
-        @pl.when(sees_last)
-        def _():
-            attend(tick, start, firsts, rows, qbuf, kbuf, vbuf, best_ref, accum_ref, finish)
-
-        @pl.when(jnp.logical_and(least < start + rows, jnp.logical_not(sees_last)))
-        def _():
-            attend(tick, start, firsts[:2], rows, qbuf, kbuf, vbuf, best_ref, accum_ref, finish)
-
-        @pl.when(least >= start + rows)
-        def _():
-            for h in range(heads):
-                finish(h, accum_ref[tick * heads + h])
+    def finish(tick, h, result):
+        obuf[tick, :, pl.ds(h * HEAD_SIZE, HEAD_SIZE)] = (result[:, :HEAD_SIZE] * pl.reciprocal(result[:, HEAD_SIZE:])).astype(obuf.dtype)
+        if h % STRIP == STRIP - 1:
+            strip_out(tick, h // STRIP).start()
+
+    def planned(tick, seen):
+        return plan(tick, index_ref[tick, me] * rows, seen, rows, qbuf, kbuf, vbuf, best_ref, accum_ref, functools.partial(finish, tick))
+
+    all_see = last_base < (index_ref[0, me] + 1) * rows
+    for tick in range(1, ticks):
+        all_see = jnp.logical_and(all_see, last_base < (index_ref[tick, me] + 1) * rows)
+
+    @pl.when(all_see)
+    def _():
+        follow([step for tick in range(ticks) for step in planned(tick, firsts)])
+
+    @pl.when(jnp.logical_not(all_see))
+    def _():
+        @pl.loop(0, ticks)
+        def _(tick):
+            start = index_ref[tick, me] * rows
+            sees_last = last_base < start + rows
+
+            @pl.when(sees_last)
+            def _():
+                follow(planned(tick, firsts))
+
+            @pl.when(jnp.logical_and(least < start + rows, jnp.logical_not(sees_last)))
+            def _():
+                follow(planned(tick, firsts[:2]))
+
+            @pl.when(least >= start + rows)
+            def _():
+                for h in range(heads):
+                    finish(tick, h, accum_ref[tick * heads + h])
 
     for tick in range(ticks):
         for strip in range(heads // STRIP):

time: 34.8 us -> 35.2 us (1.011)
  the two profiles are of different devices: /device:TPU:28 before, /device:TPU:27 now
where the time goes in v7:
time: 35.2 us; the launch traced here: 34.8 us
  Pallas kernels  34.6 us (98%)
    pallas_call x1, Pallas kernels, on_device(): pl.pallas_call(lambda *refs: gather_kernel(n_pipe, n_head, *refs), out_sh...  27.6 us
    pallas_call x1, Pallas kernels, on_device(): pl.pallas_call(lambda *refs: finish_kernel(n_pipe, n_head, *refs), out_sh...  7.09 us

profile of v7, /device:TPU:27, one launch (start us, length us, event | category | flops | bytes accessed | tf_op | source)
XLA Modules:
  0.0 34.8 jit_solution(6456004771908041165)
XLA Ops:
  0.0 27.6 %gather.1 = (bf16[2048,256]{1,0:T(8,128)(2,1)S(1)}, bf16[2048,256]{1,0:T(8,128)(2,1)S(1)}, bf16[2,256,2048]{2,1,0:T(8,128)(2,1)S(1)}, f32[32,256,128]{2,1,0:T(8,...) custom-call(s32[2,8]{1,0:T(2,128)} %refs_0_.1, bf16[2,256,2048]{2,1,0:T(8,128)(2,1)} %refs_1_.1, ...), custom_call_target="tpu_custom_call" | custom-call | tf_op jit(solution)/shard_map/gather/pallas_call | solution.py:452
  27.6 7.1 %finish.1 = bf16[2,256,2048]{2,1,0:T(8,128)(2,1)} custom-call(s32[2,8]{1,0:T(2,128)S(4)} %get-tuple-element.11.refs_0_, bf16[2048,256]{1,0:T(8,128)(2,1)S(1)} %get-tuple-element.12.refs_1_, bf16[2048,256]{1,0:T(8,128)(2,1)S(1)} %get-tuple-element.13.refs_2_, bf16[2,256,2048]{2,1,0:T(8,128)(2,1)S(1)} %get-tuple-element.14.refs_3_, ...), custom_call_target="tpu_custom_call" | custom-call | tf_op jit(solution)/shard_map/finish/pallas_call | solution.py:481

commit v8 on v6

--- a/solution.py
+++ b/solution.py
@@ -376,10 +376,6 @@
         older = jnp.where(step == 1, part(me, 0), part(side_owner(step - 2), 1))
         compute([part(own_owner(step - 1), 1), older, part(own_owner(step), 0), part(side_owner(step - 1), 0)], events(step))
 
-    for order in range(2):
-        side_wait(line - 1, order)
-    guests_pass(line - 1)
-
     for kind in range(2):
         for shift in range(1, near_heads):
             exchange(kind, 0, shift).wait_send()
@@ -414,6 +410,10 @@
         @pl.when(has_left)
         def _():
             to_left(kind, last_side, 1 - mine).wait_send()
+
+    for order in range(2):
+        side_wait(line - 1, order)
+    guests_pass(line - 1)
 
 
 def wide_join(parts, axis):

time: 34.8 us -> 34.8 us (level)
  no operation moved by 1% of the time
where the time goes in v8:
time: 34.8 us; the launch traced here: 34.6 us
  Pallas kernels  34.6 us (99%)
    pallas_call x1, Pallas kernels, on_device(): pl.pallas_call(lambda *refs: gather_kernel(n_pipe, n_head, *refs), out_sh...  27.3 us
    pallas_call x1, Pallas kernels, on_device(): pl.pallas_call(lambda *refs: finish_kernel(n_pipe, n_head, *refs), out_sh...  7.29 us

profile of v8, /device:TPU:28, one launch (start us, length us, event | category | flops | bytes accessed | tf_op | source)
XLA Modules:
  0.0 34.6 jit_solution(16929688243859010900)
XLA Ops:
  0.0 27.3 %gather.1 = (bf16[2048,256]{1,0:T(8,128)(2,1)S(1)}, bf16[2048,256]{1,0:T(8,128)(2,1)S(1)}, bf16[2,256,2048]{2,1,0:T(8,128)(2,1)S(1)}, f32[32,256,128]{2,1,0:T(8,...) custom-call(s32[2,8]{1,0:T(2,128)} %refs_0_.1, bf16[2,256,2048]{2,1,0:T(8,128)(2,1)} %refs_1_.1, ...), custom_call_target="tpu_custom_call" | custom-call | tf_op jit(solution)/shard_map/gather/pallas_call | solution.py:431
  27.3 7.3 %finish.1 = bf16[2,256,2048]{2,1,0:T(8,128)(2,1)} custom-call(s32[2,8]{1,0:T(2,128)S(4)} %get-tuple-element.11.refs_0_, bf16[2048,256]{1,0:T(8,128)(2,1)S(1)} %get-tuple-element.12.refs_1_, bf16[2048,256]{1,0:T(8,128)(2,1)S(1)} %get-tuple-element.13.refs_2_, bf16[2,256,2048]{2,1,0:T(8,128)(2,1)S(1)} %get-tuple-element.14.refs_3_, ...), custom_call_target="tpu_custom_call" | custom-call | tf_op jit(solution)/shard_map/finish/pallas_call | solution.py:460
